TPU v7x, 512 devices: a whole 4x4x16 slice. The times are simulated.
512 devices in a mesh: req: 128 (over x, z, core), tp: 4 (over y).
Axes of the slice: x: 4, y: 4, z: 16, core: 2. Of those that a mesh axis runs over, the one named last changes fastest.
Arguments:
- queries: bfloat16 [2, 128, 32, 1536], P(None, 'req', None, 'tp')
- response_kv: bfloat16 [2, 128, 2, 32, 256], P(None, 'req'), may hold values from -6 to 6
- cache_kv: bfloat16 [2, 128, 2, 384, 256], P(None, 'req'), may hold values from -6 to 6
- residual: bfloat16 [2, 128, 32, 1536], P(None, 'req')
- out_proj: bfloat16 [2, 1536, 1536], P(None, 'tp'), may hold values from -0.5 to 0.5
- norm_gain: float32 [2, 1536], replicated, may hold values from 0.25 to 1.75
- lm_head: bfloat16 [2, 131072, 1536], P(None, 'req', 'tp')
- targets: int32 [128, 32], P(None, 'tp'), may hold values from 0 to 131071
- resp_lengths: int32 [128], replicated, may hold values from 1 to 32, 2560 in all
- cache_lengths: int32 [128], P('req'), may hold values from 1 to 384, 30720 in all
- owner_slot: int32 [128], replicated, may hold values from 0 to 127, each once
- sink_count: int32 [1], replicated, may hold values from 1 to 95
- window_size: int32 [1], replicated, may hold values from 48 to 191
Outputs:
- token_logprobs: float32 [128, 32], P('req', 'tp')
- request_scores: float32 [128, 2], P('req')
Inputs may be any that keep to these rules, and one draw needn't show every extreme that they name: `resp_lengths`: live response slots are the first ones; all lengths sum to 2560. `cache_lengths`: live cache slots are the first ones; all lengths sum to 30720. `owner_slot`: A permutation of the requests.
All inputs are finite; a program needn't handle non-finite values. No bound on the sum of `cache_lengths` on one device may be relied on, other than what follows from the above.
Results may differ from a plain program's by a relative error of at most 0.0014.
Values may be sent and summed in bfloat16 or wider, within the bound.
A program may use at most 128 MiB of HBM per device.

v0:
```python
import jax
import jax.numpy as jnp
from jax import lax
from jax.sharding import PartitionSpec as P

HEADS = 12
HEAD = 128
KV_HEADS = 2
RESP = 32
CACHE = 384


def span_mask(lengths, sink_count, window_size):
    cache_pos = jnp.arange(CACHE, dtype=jnp.int32)
    slot_pos = jnp.arange(RESP, dtype=jnp.int32)
    req_count = lengths.shape[0]
    key_pos = jnp.concatenate([cache_pos[None, :], lengths[:, None] + slot_pos[None, :]], axis=1)
    key_live = jnp.concatenate(
        [cache_pos[None, :] < lengths[:, None], jnp.ones((req_count, RESP), jnp.bool_)], axis=1
    )
    query_pos = lengths[:, None] + slot_pos[None, :]
    earlier = key_pos[:, None, :] <= query_pos[:, :, None]
    inside = (key_pos[:, None, :] < sink_count[0]) | (
        query_pos[:, :, None] - key_pos[:, None, :] < window_size[0]
    )
    return key_live[:, None, :] & earlier & inside


def rms_norm(hidden, norm_gain):
    scale_inv = lax.rsqrt(jnp.mean(hidden * hidden, axis=-1, keepdims=True) + 1e-06)
    return (hidden * scale_inv * norm_gain[:, None, None, :]).astype(jnp.bfloat16)


def per_device(
    queries,
    response_kv,
    cache_kv,
    residual,
    out_proj,
    norm_gain,
    lm_head,
    targets,
    resp_lengths,
    cache_lengths,
    owner_slot,
    sink_count,
    window_size,
):
    tp_size = lax.axis_size("tp")
    tp_index = lax.axis_index("tp")
    req_index = lax.axis_index("req")
    local_reqs = queries.shape[1]
    local_heads = HEADS // tp_size
    group_size = HEADS // KV_HEADS
    kv_index = tp_index * local_heads // group_size
    quarter = RESP // tp_size
    cache_head = lax.dynamic_slice_in_dim(cache_kv, kv_index * HEAD, HEAD, axis=4)
    resp_head = lax.dynamic_slice_in_dim(response_kv, kv_index * HEAD, HEAD, axis=4)
    key_rows = jnp.concatenate([cache_head[:, :, 0], resp_head[:, :, 0]], axis=2)
    value_rows = jnp.concatenate([cache_head[:, :, 1], resp_head[:, :, 1]], axis=2)
    query_heads = queries.reshape(2, local_reqs, RESP, local_heads, HEAD)
    scores = jnp.einsum(
        "mrshd,mrkd->mrhsk", query_heads, key_rows, preferred_element_type=jnp.float32
    ) * HEAD ** (-0.5)
    allowed = span_mask(cache_lengths, sink_count, window_size)[None, :, None]
    masked = jnp.where(allowed, scores, -jnp.inf)
    row_peak = jnp.max(masked, axis=-1, keepdims=True)
    weights = jnp.exp(masked - row_peak)
    weights = (weights / jnp.sum(weights, axis=-1, keepdims=True)).astype(jnp.bfloat16)
    attended = jnp.einsum(
        "mrhsk,mrkd->mrshd", weights, value_rows, preferred_element_type=jnp.float32
    )
    attended = attended.astype(jnp.bfloat16).reshape(2, local_reqs, RESP, local_heads * HEAD)
    partial_value = jnp.einsum(
        "mrsf,mfd->mrsd", attended, out_proj, preferred_element_type=jnp.float32
    )
    start_slot = tp_index * quarter
    projected = lax.dynamic_slice_in_dim(lax.psum(partial_value, "tp"), start_slot, quarter, axis=2)
    own_residual = lax.dynamic_slice_in_dim(residual, start_slot, quarter, axis=2)
    hidden = own_residual.astype(jnp.float32) + projected
    normed = rms_norm(hidden, norm_gain)
    flat_rows = normed.reshape(2, local_reqs * quarter, normed.shape[3])
    full_head = lax.all_gather(lm_head, "tp", axis=2, tiled=True)
    vocab_rows = full_head.shape[1]
    vocab_start = req_index * vocab_rows
    flat_targets = targets.reshape(-1)
    total_rows = flat_targets.shape[0]
    requests = total_rows // quarter
    logits = jnp.einsum(
        "mnd,mvd->mnv",
        lax.all_gather(flat_rows, "req", axis=1, tiled=True),
        full_head,
        preferred_element_type=jnp.float32,
    )
    block_peak = jnp.max(logits, axis=-1)
    block_total = jnp.sum(jnp.exp(logits - block_peak[..., None]), axis=-1)
    wanted = flat_targets - vocab_start
    target_hits = jnp.arange(vocab_rows, dtype=jnp.int32)[None, None, :] == wanted[None, :, None]
    block_pick = jnp.sum(jnp.where(target_hits, logits, 0.0), axis=-1)
    peak_all = block_peak
    total_all = block_total
    picked_all = block_pick
    peak_all = peak_all.reshape(2, requests, quarter)
    total_all = total_all.reshape(2, requests, quarter)
    picked_all = picked_all.reshape(2, requests, quarter)
    row_order = (
        jnp.zeros((requests,), jnp.int32).at[owner_slot].set(jnp.arange(requests, dtype=jnp.int32))
    )
    owned_reqs = lax.dynamic_slice_in_dim(row_order, req_index * local_reqs, local_reqs)
    vocab_top = lax.pmax(peak_all, "req")
    exp_total, picked = lax.psum((total_all * jnp.exp(peak_all - vocab_top), picked_all), "req")
    logprob = (picked - (vocab_top + jnp.log(exp_total)))[:, owned_reqs]
    lengths_owned = resp_lengths[owned_reqs]
    live_slots = (start_slot + jnp.arange(quarter, dtype=jnp.int32))[None, :] < lengths_owned[
        :, None
    ]
    policy = jnp.where(live_slots, logprob[0], 0.0)
    log_ratio = jnp.where(live_slots, logprob[0] - logprob[1], 0.0)
    policy_total, ratio_total = lax.psum(
        (jnp.sum(policy, axis=1), jnp.sum(log_ratio, axis=1)), "tp"
    )
    counts = lengths_owned.astype(jnp.float32)
    request_scores = jnp.stack([policy_total / counts, ratio_total / counts], axis=1)
    return (policy, request_scores)


def solution(mesh):
    in_specs = (
        P(None, "req", None, "tp"),
        P(None, "req", None, None, None),
        P(None, "req", None, None, None),
        P(None, "req", None, None),
        P(None, "tp", None),
        P(),
        P(None, "req", "tp"),
        P(None, "tp"),
        P(),
        P("req"),
        P(),
        P(),
        P(),
    )
    out_specs = (P("req", "tp"), P("req", None))
    return jax.shard_map(
        per_device, mesh=mesh, in_specs=in_specs, out_specs=out_specs, check_vma=False
    )
```

profile of v0, /device:TPU:8, one launch (start us, length us, event | category | flops | bytes accessed | tf_op | source)
XLA Modules:
  0.0 1325.8 jit_solution(16412632593061100903)
XLA Ops:
  7.3 1.2 dynamic-slice_bitcast_fusion
  8.5 0.8 dynamic-slice_bitcast_fusion.2
  11.3 0.8 reshape.303
  12.1 0.1 fusion.12
  12.2 0.3 fusion.23
  12.6 0.2 fusion.5
  12.8 0.3 fusion.4
  13.1 0.1 reshape.305
  13.2 1.3 convolution_bitcast_fusion
  14.5 0.7 all-gather.4.cloned.1.call-update
  15.3 60.6 %all-reduce.5.cloned.1.call-done = f32[2,1,32,1536]{3,2,0,1:T(8,128)} async-done(((f32[2,1,32,1536]{3,2,0,1:T(8,128)}), f32[2,1,32,1536]{3,2,0,1:T(8,128)}) %all-reduce.5.cloned.1.call-update) | async-done | bytes 393232 | tf_op jit(solution)/shard_map/psum | solution.py:78
  75.8 1.0 multiply_reduce_fusion
  76.9 1.6 multiply_convert_fusion
  78.5 0.1 copy.19
  78.6 0.1 sub.65
  78.7 1.0 scatter_custom_fusion
  79.7 0.6 dynamic_slice.15
  82.2 0.6 dynamic-slice.5
  83.5 0.8 iota_compare_fusion
  84.3 68.4 %all-gather.4.cloned.1.call-done = bf16[2,1024,1536]{2,1,0:T(8,128)(2,1)} async-done(((bf16[2,1024,384]{2,1,0:T(8,128)(2,1)}), bf16[2,1024,1536]{2,1,0:T(8,128)(2,1)}) %all-gather.4.cloned.1.call-update) | async-done | bytes 6291472 | tf_op jit(solution)/shard_map/all_gather | solution.py:83
  152.7 149.5 %all-gather.6.cloned.1.call-done = bf16[2,1,1024,1536]{3,2,0,1:T(8,128)(2,1)} async-done(((bf16[2,1,8,1536]{3,2,0,1:T(8,128)(2,1)}), bf16[2,1,1024,1536]{3,2,0,1:T(8,128)(2,1)}) %all-gather.6.cloned.1.call-update) | async-done | bytes 6291472 | tf_op jit(solution)/shard_map/all_gather | solution.py:91
  302.2 12.7 fusion.24
  314.9 0.1 reshape.308
  315.0 5.1 exponential_reduce_fusion
  320.1 0.8 reshape.309
  320.9 493.2 %pmax.7 = f32[2,128,8]{2,1,0:T(8,128)S(1)} all-reduce(f32[2,128,8]{2,1,0:T(8,128)S(1)} %reshape.308), channel_id=1, replica_groups=mesh['req'=128,'tp'=4] {'req'}, use_global_device_ids=true, to_apply=%region_8.9 | all-reduce | flops 2048 | bytes 16384 | tf_op jit(solution)/shard_map/pmax | solution.py:110
  814.1 0.1 reshape.307
  814.2 490.9 %all-reduce.1 = (f32[2,128,8]{2,1,0:T(8,128)S(1)}, f32[2,128,8]{2,1,0:T(8,128)S(1)}) all-reduce(f32[2,128,8]{2,1,0:T(8,128)S(1)} %reshape.307, f32[2,128,8]{2,1,0:T(8,128)S(1)} %exponential_multiply_fusion), channel_id=1, replica_groups=mesh['req'=128,'tp'=4] {'req'}, use_global_device_ids=true, to_apply=%region_6.7 | all-reduce | flops 4096 | bytes 32768 | tf_op jit(solution)/shard_map/psum | solution.py:111
  1305.2 1.2 fusion.17
  1306.4 1.7 fusion.22
  1308.1 9.3 all-reduce.2
  1318.7 0.6 pad_maximum_fusion
  (31 shorter events, 0.3 us)
Async XLA Ops:
  7.2 6.0 copy-start
  7.2 68.7 %copy-start.1 = (bf16[2,1,32,1536]{3,2,1,0:T(8,128)(2,1)S(1)}, bf16[2,1,32,1536]{3,2,1,0:T(8,128)(2,1)}, u32[]{:S(2)}) copy-start(bf16[2,1,32,1536]{3,2,1,0:T(8,128)(2,1)} %param.16) | copy-start | bytes 589828
  7.2 69.7 %copy-start.2 = (f32[2,1536]{1,0:T(2,128)S(1)}, f32[2,1536]{1,0:T(2,128)}, u32[]{:S(2)}) copy-start(f32[2,1536]{1,0:T(2,128)} %param.18) | copy-start | bytes 36868
  7.2 71.3 %copy-start.3 = (s32[128,8]{0,1:T(8,128)S(1)}, s32[128,8]{0,1:T(8,128)}, u32[]{:S(2)}) copy-start(s32[128,8]{0,1:T(8,128)} %param.20) | copy-start | bytes 12292
  7.2 71.5 %copy-start.4 = (s32[128]{0:T(128)S(1)}, s32[128]{0:T(128)}, u32[]{:S(2)}) copy-start(s32[128]{0:T(128)} %param.23) | copy-start | bytes 1540
  7.2 75.0 %copy-start.5 = (s32[128]{0:T(128)S(1)}, s32[128]{0:T(128)}, u32[]{:S(2)}) copy-start(s32[128]{0:T(128)} %param.21) | copy-start | bytes 1540
  7.2 68.6 %all-reduce.5.cloned.1.call-start = ((), (), s32[]{:S(2)}) async-start(), calls=%async_computation | async-start | bytes 786432 | tf_op jit(solution)/shard_map/psum | solution.py:78
  14.4 138.2 %all-gather.4.cloned.1.call-start = ((), (), s32[]{:S(2)}) async-start(), calls=%async_computation.1 | async-start | bytes 7864320 | tf_op jit(solution)/shard_map/all_gather | solution.py:83
  15.2 287.0 %all-gather.6.cloned.1.call-start = ((), (), s32[]{:S(2)}) async-start(), calls=%async_computation.2 | async-start | bytes 6340608 | tf_op jit(solution)/shard_map/all_gather | solution.py:91
Sparse Core Ops, SparseCore 0:
  14.6 61.2 all-reduce.4
  78.2 74.4 all-gather.3
  156.4 145.7 all-gather.5
where the time goes:
time: 1330 us
  blocking collectives  993 us (75%)
  waiting for transfers between devices  279 us (21%)
  between operations  19.9 us (1%)
  matrix products  14.6 us (1%)
    pmax x1, blocking collectives, per_device(): vocab_top = lax.pmax(peak_all, 'req')  493 us
    psum x1, blocking collectives, per_device(): lax.psum((total_all * jnp.exp(peak_all - vocab_top), picked_all), 'req')  491 us
    all_gather x1, waiting for transfers between devices, per_device(): lax.all_gather(flat_rows, 'req', axis=1, tiled=True)  149 us
    all_gather x1, waiting for transfers between devices, per_device(): full_head = lax.all_gather(lm_head, 'tp', axis=2, tiled=True)  68.4 us
    psum x1, waiting for transfers between devices, per_device(): lax.psum(partial_value, 'tp')  60.6 us
  transfers between devices with their start and end apart: 3, of which 3 were waited for; matrix products, arithmetic and copies ran while one was open for 0% of the time, Pallas kernels for 0%

commit v1 on v0

--- a/solution.py
+++ b/solution.py
@@ -88,7 +88,9 @@
     requests = total_rows // quarter
     logits = jnp.einsum(
         "mnd,mvd->mnv",
-        lax.all_gather(flat_rows, "req", axis=1, tiled=True),
+        jnp.concatenate(
+            lax.all_to_all(jnp.stack([flat_rows] * lax.axis_size("req")), "req", 0, 0), axis=1
+        ),
         full_head,
         preferred_element_type=jnp.float32,
     )

time: 1330 us -> 1400 us (1.053)
  waiting for transfers between devices: 279 us -> 332 us
  starting transfers between devices: 0.12 us -> 17.3 us
    all_to_all x0 -> x1, waiting for transfers between devices: none -> 199 us  [per_device(): lax.all_to_all(jnp.stack([flat_rows] * lax.axis_size('req')), 'req', 0, 0)]
    all_gather x1 -> x0, waiting for transfers between devices: 149 us -> none  [per_device(): lax.all_gather(flat_rows, 'req', axis=1, tiled=True)]
    all_to_all x0 -> x1, starting transfers between devices: none -> 17.3 us  [per_device(): lax.all_to_all(jnp.stack([flat_rows] * lax.axis_size('req')), 'req', 0, 0)]
where the time goes in v1:
time: 1400 us
  blocking collectives  992 us (71%)
  waiting for transfers between devices  332 us (24%)
  between operations  20.2 us (1%)
  starting transfers between devices  17.3 us (1%)
  matrix products  14.6 us (1%)
    psum x1, blocking collectives, per_device(): lax.psum((total_all * jnp.exp(peak_all - vocab_top), picked_all), 'req')  491 us
    pmax x1, blocking collectives, per_device(): vocab_top = lax.pmax(peak_all, 'req')  491 us
    all_to_all x1, waiting for transfers between devices, per_device(): lax.all_to_all(jnp.stack([flat_rows] * lax.axis_size('req')), 'req', 0, 0)  199 us
    all_gather x1, waiting for transfers between devices, per_device(): full_head = lax.all_gather(lm_head, 'tp', axis=2, tiled=True)  70.6 us
    psum x1, waiting for transfers between devices, per_device(): lax.psum(partial_value, 'tp')  61.4 us
  transfers between devices with their start and end apart: 3, of which 3 were waited for; matrix products, arithmetic and copies ran while one was open for 0% of the time, Pallas kernels for 0%

profile of v1, /device:TPU:8, one launch (start us, length us, event | category | flops | bytes accessed | tf_op | source)
XLA Modules:
  0.0 1397.5 jit_solution(1308066047407845473)
XLA Ops:
  7.3 1.2 dynamic-slice_bitcast_fusion
  8.5 0.8 dynamic-slice_bitcast_fusion.2
  11.2 0.8 reshape.308
  12.1 0.1 fusion.13
  12.2 0.3 fusion.25
  12.5 0.2 fusion.6
  12.7 0.3 fusion.5
  13.1 1.3 convolution_bitcast_fusion
  14.4 61.4 %all-reduce.5.cloned.1.call-done = f32[2,1,32,1536]{3,2,0,1:T(8,128)} async-done(((f32[2,1,32,1536]{3,2,0,1:T(8,128)}), f32[2,1,32,1536]{3,2,0,1:T(8,128)}) %all-reduce.5.cloned.1.call-update) | async-done | bytes 393232 | tf_op jit(solution)/shard_map/psum | solution.py:78
  75.8 1.0 multiply_reduce_fusion
  76.8 1.0 fusion.14
  77.8 3.4 stack.12
  81.3 17.3 %all-to-all-start = ((bf16[128,2,8,1536]{3,2,1,0:T(8,128)(2,1)}), bf16[128,2,8,1536]{3,2,1,0:T(8,128)(2,1)}, u32[]{:S(2)}, u32[]{:S(2)}) async-start(bf16[128,2,8,1536]{3,2,1,0:T(8,128)(2,1)} %stack.12), calls=%async_computation | async-start | bytes 12582912 | tf_op jit(solution)/shard_map/all_to_all | solution.py:92
  98.6 0.7 all-gather.2.cloned.1.call-update
  99.3 0.1 copy.25
  99.5 1.0 scatter_custom_fusion
  100.5 0.6 dynamic_slice.15
  103.1 0.6 dynamic-slice.5
  104.3 0.8 iota_compare_fusion
  105.1 70.6 %all-gather.2.cloned.1.call-done = bf16[2,1024,1536]{2,1,0:T(8,128)(2,1)} async-done(((bf16[2,1024,384]{2,1,0:T(8,128)(2,1)}), bf16[2,1024,1536]{2,1,0:T(8,128)(2,1)}) %all-gather.2.cloned.1.call-update) | async-done | bytes 6291472 | tf_op jit(solution)/shard_map/all_gather | solution.py:83
  175.7 199.5 %all-to-all-done = bf16[128,2,8,1536]{3,2,1,0:T(8,128)(2,1)} async-done(((bf16[128,2,8,1536]{3,2,1,0:T(8,128)(2,1)}), bf16[128,2,8,1536]{3,2,1,0:T(8,128)(2,1)}, u32[]{:S(2)}, u32[]{:S(2)}) %all-to-all-start) | async-done | bytes 6291488 | tf_op jit(solution)/shard_map/all_to_all | solution.py:92
  375.2 12.7 fusion.26
  387.9 0.1 reshape.314
  388.0 5.1 exponential_reduce_fusion
  393.1 0.8 reshape.315
  393.9 490.9 %pmax.7 = f32[2,128,8]{2,1,0:T(8,128)S(1)} all-reduce(f32[2,128,8]{2,1,0:T(8,128)S(1)} %reshape.314), channel_id=1, replica_groups=mesh['req'=128,'tp'=4] {'req'}, use_global_device_ids=true, to_apply=%region_8.9 | all-reduce | flops 2048 | bytes 16384 | tf_op jit(solution)/shard_map/pmax | solution.py:112
  884.7 0.1 reshape.313
  884.9 490.9 %all-reduce.1 = (f32[2,128,8]{2,1,0:T(8,128)S(1)}, f32[2,128,8]{2,1,0:T(8,128)S(1)}) all-reduce(f32[2,128,8]{2,1,0:T(8,128)S(1)} %reshape.313, f32[2,128,8]{2,1,0:T(8,128)S(1)} %exponential_multiply_fusion), channel_id=1, replica_groups=mesh['req'=128,'tp'=4] {'req'}, use_global_device_ids=true, to_apply=%region_6.7 | all-reduce | flops 4096 | bytes 32768 | tf_op jit(solution)/shard_map/psum | solution.py:113
  1375.8 1.2 fusion.19
  1377.0 1.7 fusion.24
  1378.7 10.0 all-reduce.2
  1390.1 0.6 pad_maximum_fusion
  (31 shorter events, 0.4 us)
Async XLA Ops:
  7.2 6.0 copy-start
  7.2 68.6 %copy-start.1 = (bf16[2,1,32,1536]{3,2,1,0:T(8,128)(2,1)S(1)}, bf16[2,1,32,1536]{3,2,1,0:T(8,128)(2,1)}, u32[]{:S(2)}) copy-start(bf16[2,1,32,1536]{3,2,1,0:T(8,128)(2,1)} %param.16) | copy-start | bytes 589828
  7.2 69.6 %copy-start.2 = (f32[2,1536]{1,0:T(2,128)S(1)}, f32[2,1536]{1,0:T(2,128)}, u32[]{:S(2)}) copy-start(f32[2,1536]{1,0:T(2,128)} %param.18) | copy-start | bytes 36868
  7.2 68.6 %all-reduce.5.cloned.1.call-start = ((), (), s32[]{:S(2)}) async-start(), calls=%async_computation.1 | async-start | bytes 786432 | tf_op jit(solution)/shard_map/psum | solution.py:78
  81.3 18.0 %copy-start.3 = (s32[128,8]{0,1:T(8,128)S(1)}, s32[128,8]{0,1:T(8,128)}, u32[]{:S(2)}) copy-start(s32[128,8]{0,1:T(8,128)} %param.20) | copy-start | bytes 12292
  81.3 18.2 %copy-start.4 = (s32[128]{0:T(128)S(1)}, s32[128]{0:T(128)}, u32[]{:S(2)}) copy-start(s32[128]{0:T(128)} %param.23) | copy-start | bytes 1540
  81.3 21.8 %copy-start.5 = (s32[128]{0:T(128)S(1)}, s32[128]{0:T(128)}, u32[]{:S(2)}) copy-start(s32[128]{0:T(128)} %param.21) | copy-start | bytes 1540
  81.3 293.9 %all-to-all-start = ((bf16[128,2,8,1536]{3,2,1,0:T(8,128)(2,1)}), bf16[128,2,8,1536]{3,2,1,0:T(8,128)(2,1)}, u32[]{:S(2)}, u32[]{:S(2)}) async-start(bf16[128,2,8,1536]{3,2,1,0:T(8,128)(2,1)} %stack.12), calls=%async_computation | async-start | bytes 12582912 | tf_op jit(solution)/shard_map/all_to_all | solution.py:92
  98.5 77.2 %all-gather.2.cloned.1.call-start = ((), (), s32[]{:S(2)}) async-start(), calls=%async_computation.2 | async-start | bytes 7864320 | tf_op jit(solution)/shard_map/all_gather | solution.py:83
Sparse Core Ops, SparseCore 0:
  14.6 61.2 all-reduce.4
  101.7 73.9 all-gather.1
